TPU v7x, 256 devices: a whole 4x4x8 slice. The times are simulated.
256 devices in a mesh: box: 32 (over x, z), pencil: 8 (over y, core).
Axes of the slice: x: 4, y: 4, z: 8, core: 2. Of those that a mesh axis runs over, the one named last changes fastest.
Arguments:
- previous: bfloat16 [32, 256, 256, 128], P('box', 'pencil'), may hold values from -48 to 48
- source: bfloat16 [32, 256, 256, 128], P('box', 'pencil'), may hold values from -48 to 48
- neighbor: int32 [32, 2, 16], replicated, may hold values from 0 to 31, as said below
- depth: int32 [32, 2, 16], replicated, may hold values from 1 to 8
- wall: int32 [32, 2, 256], P('box', None, 'pencil'), may hold values 0 or 1
Outputs:
- solution: float32 [32, 256, 256, 128], P('box', 'pencil')
Inputs may be any that keep to these rules, and one draw needn't show every extreme that they name: For each face and segment, neighbor[:, face, segment] is a permutation of the 32 boxes in which no box names itself.
All inputs are finite; a program needn't handle non-finite values. No bound on the sum of `wall` on one device may be relied on, other than what follows from the above.
Results may differ from a plain program's by a relative error of at most 0.014.
Values may be sent and summed in bfloat16 or wider, within the bound.
A program may use at most 64 MiB of HBM per device.

v0:
```python
import jax
import jax.numpy as jnp
from jax import lax
from jax.sharding import PartitionSpec as P

W = 8
ITERS = 2


REFLECT = 0.6
TIMESTEP = 64.0


def sine_table(length):
    ordinal = jnp.arange(length, dtype=jnp.float32) + 1.0
    phase_angle = jnp.pi * ordinal[:, None] * ordinal[None, :] / (length + 1.0)
    return (jnp.sqrt(2.0 / (length + 1.0)) * jnp.sin(phase_angle)).astype(jnp.bfloat16)


def eigen_values(length):
    ordinal = jnp.arange(length, dtype=jnp.float32) + 1.0
    return 2.0 - 2.0 * jnp.cos(jnp.pi * ordinal / (length + 1.0))


def shards(previous, source, neighbor, depth, wall):
    pencils = lax.axis_size("pencil")
    pencil_index = lax.axis_index("pencil")
    box_index = lax.axis_index("box")
    plane_count = previous.shape[1]
    column_count = previous.shape[2]
    depth_count = previous.shape[3]
    length_all = plane_count * pencils
    segment_count = neighbor.shape[2]
    segment_length = length_all // segment_count
    length_table = sine_table(length_all)
    width_table = sine_table(column_count)
    depth_table = sine_table(depth_count)
    length_eigen = eigen_values(length_all)
    width_eigen = eigen_values(column_count)
    depth_eigen = eigen_values(depth_count)
    forcing = previous[0].astype(jnp.float32) + source[0].astype(jnp.float32)
    positions = jnp.arange(plane_count, dtype=jnp.int32)
    global_planes = pencil_index * plane_count + positions
    segment_hit = (global_planes // segment_length)[:, None] == jnp.arange(
        segment_count, dtype=jnp.int32
    )[None, :]
    own_lists = lax.dynamic_index_in_dim(neighbor, box_index, 0, keepdims=False)
    own_depths = lax.dynamic_index_in_dim(depth, box_index, 0, keepdims=False)
    donor_box = jnp.sum(jnp.where(segment_hit[None], own_lists[:, None, :], 0), axis=2)
    donor_depth = jnp.sum(jnp.where(segment_hit[None], own_depths[:, None, :], 0), axis=2)
    end_planes = ((global_planes == 0) | (global_planes == length_all - 1)).astype(jnp.float32)[
        :, None, None
    ]
    wall_local = wall[0]
    current = previous[0]
    solved = None
    for iteration in range(ITERS):
        iterate = current.astype(jnp.float32)
        high_band = current[:, column_count - 1 - W : column_count - 1, :][:, ::-1, :]
        low_band = current[:, 1 : W + 1, :]
        export = jnp.concatenate([high_band, low_band], axis=1)
        gathered = lax.all_gather(export, "box", axis=0, tiled=True)
        low_import = gathered[donor_box[0] * plane_count + positions, donor_depth[0] - 1, :]
        high_import = gathered[donor_box[1] * plane_count + positions, W + donor_depth[1] - 1, :]
        low_ghost = jnp.where(
            wall_local[0][:, None] == 1, REFLECT * iterate[:, 0, :], low_import.astype(jnp.float32)
        )
        high_ghost = jnp.where(
            wall_local[1][:, None] == 1,
            REFLECT * iterate[:, column_count - 1, :],
            high_import.astype(jnp.float32),
        )
        boundary = jnp.zeros_like(iterate)
        boundary = boundary.at[:, 0, :].add(low_ghost)
        boundary = boundary.at[:, column_count - 1, :].add(high_ghost)
        boundary = boundary + end_planes * (REFLECT * iterate)
        boundary = boundary.at[:, :, 0].add(REFLECT * iterate[:, :, 0])
        boundary = boundary.at[:, :, depth_count - 1].add(REFLECT * iterate[:, :, depth_count - 1])
        right_side = (forcing + TIMESTEP * boundary).astype(jnp.bfloat16)
        first_pass = jnp.einsum(
            "xyz,zk->xyk", right_side, depth_table, preferred_element_type=jnp.float32
        ).astype(jnp.bfloat16)
        second_pass = jnp.einsum(
            "xyz,yk->xkz", first_pass, width_table, preferred_element_type=jnp.float32
        ).astype(jnp.bfloat16)
        spread = lax.all_to_all(second_pass, "pencil", split_axis=1, concat_axis=0, tiled=True)
        width_part = spread.shape[1]
        width_slice = lax.dynamic_slice_in_dim(width_eigen, pencil_index * width_part, width_part)
        spectrum = 1.0 + TIMESTEP * (
            length_eigen[:, None, None] + width_slice[None, :, None] + depth_eigen[None, None, :]
        )
        third_pass = jnp.einsum(
            "xyz,xk->kyz", spread, length_table, preferred_element_type=jnp.float32
        )
        fourth_pass = (third_pass / spectrum).astype(jnp.bfloat16)
        fifth_pass = jnp.einsum(
            "xyz,xk->kyz", fourth_pass, length_table, preferred_element_type=jnp.float32
        ).astype(jnp.bfloat16)
        returned = lax.all_to_all(fifth_pass, "pencil", split_axis=0, concat_axis=1, tiled=True)
        sixth_pass = jnp.einsum(
            "xyz,yk->xkz", returned, width_table, preferred_element_type=jnp.float32
        ).astype(jnp.bfloat16)
        solved = jnp.einsum(
            "xyz,zk->xyk", sixth_pass, depth_table, preferred_element_type=jnp.float32
        )
        current = solved.astype(jnp.bfloat16)
    return solved[None]


def solution(mesh):
    placed = (
        P("box", "pencil", None, None),
        P("box", "pencil", None, None),
        P(),
        P(),
        P("box", None, "pencil"),
    )
    return jax.shard_map(
        shards,
        mesh=mesh,
        in_specs=placed,
        out_specs=P("box", "pencil", None, None),
        check_vma=False,
    )
```

profile of v0, /device:TPU:1, one launch (start us, length us, event | category | flops | bytes accessed | tf_op | source)
XLA Modules:
  0.0 455.1 jit_solution(6380604464187133774)
XLA Ops:
  10.2 4.2 bitcast_convert_fusion
  14.5 77.5 %all-gather.3.cloned.1.call-done = bf16[1024,16,128]{2,1,0:T(8,128)(2,1)} async-done(((bf16[32,16,128]{2,1,0:T(8,128)(2,1)}), bf16[1024,16,128]{2,1,0:T(8,128)(2,1)}) %all-gather.3.cloned.1.call-update) | async-done | bytes 4194320 | tf_op jit(solution)/shard_map/all_gather | solution.py:62
  100.0 3.0 multiply_add_fusion.2
  107.5 10.9 %scatter-add.30 = f32[32,256,128]{2,1,0:T(8,128)} dynamic-update-slice(f32[32,256,128]{2,1,0:T(8,128)} %copy-done.1, f32[32,256,1]{2,1,0:T(8,128)} %fusion.3, s32[]{:T(128)} %constant.259.clone.1, s32[]{:T(128)} %constant.259.clone.1, s32[]{:T(128)} %constant.259.clone.1) | dynamic-update-slice | bytes 65540 | tf_op jit(solution)/shard_map/scatter-add | solution.py:77
  118.5 7.7 %fusion.2 = f32[32,256,1]{2,1,0:T(8,128)} fusion(f32[32,256,128]{2,1,0:T(8,128)} %bitcast_convert_fusion, f32[32,256,128]{2,1,0:T(8,128)} %scatter-add.30), kind=kLoop, calls=%fused_computation.9 | loop fusion | flops 16384 | bytes 98304 | tf_op jit(solution)/shard_map/add | solution.py:78
  126.1 13.0 %scatter-add.31 = f32[32,256,128]{2,1,0:T(8,128)} dynamic-update-slice(f32[32,256,128]{2,1,0:T(8,128)} %scatter-add.30, f32[32,256,1]{2,1,0:T(8,128)} %fusion.2, s32[]{:T(128)} %constant.259.clone.1, s32[]{:T(128)} %constant.259.clone.1, s32[]{:T(128)} %constant.270.clone.1) | dynamic-update-slice | bytes 65540 | tf_op jit(solution)/shard_map/scatter-add | solution.py:78
  139.1 6.7 %convert_bitcast_fusion.1 = bf16[32,256,128]{2,1,0:T(8,128)(2,1)} fusion(f32[32,256,128]{2,1,0:T(8,128)} %scatter-add.31, bf16[1,32,256,128]{3,2,1,0:T(8,128)(2,1)} %param.22, f32[256]{0:T(256)S(1)} %get-tuple-element.119, f32[256]{0:T(256)S(1)} %get-tuple-element.120, f32[128]{0:T(128)S(1)} %get-tuple-element.121, f32[128]{0:T(128)S(1)} %get-tuple-element.122, ...), kind=kOutput, calls=%fused_computation.38 | convolution fusion | flops 814022656 | bytes 10488832 | tf_op jit(solution)/shard_map/xyz,yk->xkz/dot_general | solution.py:83
  145.9 4.3 copy.28
  150.1 8.4 %all-to-all-start = ((bf16[32,256,128]{2,0,1:T(8,128)(2,1)}), bf16[32,256,128]{2,0,1:T(8,128)(2,1)}, u32[]{:S(2)}, u32[]{:S(2)}) async-start(bf16[32,256,128]{2,0,1:T(8,128)(2,1)} %copy.28), calls=%async_computation | async-start | bytes 4194304 | tf_op jit(solution)/shard_map/all_to_all | solution.py:86
  159.0 25.9 %all-to-all-done = bf16[32,256,128]{2,0,1:T(8,128)(2,1)} async-done(((bf16[32,256,128]{2,0,1:T(8,128)(2,1)}), bf16[32,256,128]{2,0,1:T(8,128)(2,1)}, u32[]{:S(2)}, u32[]{:S(2)}) %all-to-all-start) | async-done | bytes 2097184 | tf_op jit(solution)/shard_map/all_to_all | solution.py:86
  184.9 3.7 copy.30
  188.6 6.9 %fusion.32 = bf16[256,32,128]{2,0,1:T(8,128)(2,1)} fusion(f32[128]{0:T(128)S(1)} %multiply_subtract_fusion.1, f32[256,32]{0,1:T(8,128)S(1)} %broadcast_add_fusion, bf16[256,32,128]{2,1,0:T(8,128)(2,1)} %bitcast.148, f32[256]{0:T(256)S(1)} %get-tuple-element.119, f32[256]{0:T(256)S(1)} %get-tuple-element.120), kind=kOutput, calls=%fused_computation.47 | convolution fusion | flops 1080557568 | bytes 4229632 | tf_op jit(solution)/shard_map/xyz,xk->kyz/dot_general | solution.py:96
  198.4 29.8 %all_to_all.72 = bf16[256,32,128]{2,1,0:T(8,128)(2,1)S(1)} all-to-all(bf16[256,32,128]{2,1,0:T(8,128)(2,1)S(1)} %copy.32), channel_id=1, replica_groups=mesh['box'=32,'pencil'=8] {'pencil'}, dimensions={0} | all-to-all | bytes 4194304 | tf_op jit(solution)/shard_map/all_to_all | solution.py:99
  230.1 6.5 %fusion.171 = (f32[32,256,128]{2,1,0:T(8,128)}, bf16[32,256,128]{2,1,0:T(8,128)(2,1)}) fusion(f32[128]{0:T(128)S(1)} %get-tuple-element.121, f32[128]{0:T(128)S(1)} %get-tuple-element.122, bf16[32,256,128]{2,1,0:T(8,128)(2,1)} %bitcast.142, f32[256]{0:T(256)S(1)} %get-tuple-element.119, f32[256]{0:T(256)S(1)} %get-tuple-element.120), kind=kOutput, calls=%fused_computation.160 | convolution fusion | flops 808779776 | bytes 8391680 | tf_op jit(solution)/shard_map/xyz,zk->xyk/dot_general | solution.py:103
  238.4 73.7 %all-gather.5.cloned.1.call-done = bf16[1024,16,128]{2,1,0:T(8,128)(2,1)} async-done(((bf16[32,16,128]{2,1,0:T(8,128)(2,1)}), bf16[1024,16,128]{2,1,0:T(8,128)(2,1)}) %all-gather.5.cloned.1.call-update) | async-done | bytes 4194320 | tf_op jit(solution)/shard_map/all_gather | solution.py:62
  320.1 3.7 multiply_add_fusion
  328.3 10.9 %scatter-add.36 = f32[32,256,128]{2,1,0:T(8,128)} dynamic-update-slice(f32[32,256,128]{2,1,0:T(8,128)} %copy-done, f32[32,256,1]{2,1,0:T(8,128)} %fusion.1, s32[]{:T(128)} %constant.259.clone.1, s32[]{:T(128)} %constant.259.clone.1, s32[]{:T(128)} %constant.259.clone.1) | dynamic-update-slice | bytes 65540 | tf_op jit(solution)/shard_map/scatter-add | solution.py:77
  339.3 7.7 %fusion = f32[32,256,1]{2,1,0:T(8,128)} fusion(f32[32,256,128]{2,1,0:T(8,128)} %get-tuple-element.115, f32[32,256,128]{2,1,0:T(8,128)} %scatter-add.36), kind=kLoop, calls=%fused_computation.5 | loop fusion | flops 16384 | bytes 98304 | tf_op jit(solution)/shard_map/add | solution.py:78
  346.9 13.0 %scatter-add.39 = f32[32,256,128]{2,1,0:T(8,128)} dynamic-update-slice(f32[32,256,128]{2,1,0:T(8,128)} %scatter-add.36, f32[32,256,1]{2,1,0:T(8,128)} %fusion, s32[]{:T(128)} %constant.259.clone.1, s32[]{:T(128)} %constant.259.clone.1, s32[]{:T(128)} %constant.270.clone.1) | dynamic-update-slice | bytes 65540 | tf_op jit(solution)/shard_map/scatter-add | solution.py:78
  359.9 6.7 %convert_bitcast_fusion = bf16[32,256,128]{2,1,0:T(8,128)(2,1)} fusion(f32[32,256,128]{2,1,0:T(8,128)} %scatter-add.39, bf16[1,32,256,128]{3,2,1,0:T(8,128)(2,1)} %param.22, f32[256]{0:T(256)S(1)} %get-tuple-element.119, f32[256]{0:T(256)S(1)} %get-tuple-element.120, f32[128]{0:T(128)S(1)} %get-tuple-element.121, f32[128]{0:T(128)S(1)} %get-tuple-element.122, ...), kind=kOutput, calls=%fused_computation.33 | convolution fusion | flops 814022656 | bytes 10488832 | tf_op jit(solution)/shard_map/xyz,yk->xkz/dot_general | solution.py:83
  369.6 34.7 %all_to_all.73 = bf16[32,256,128]{2,0,1:T(8,128)(2,1)S(1)} all-to-all(bf16[32,256,128]{2,0,1:T(8,128)(2,1)S(1)} %copy.34), channel_id=1, replica_groups=mesh['box'=32,'pencil'=8] {'pencil'}, dimensions={1} | all-to-all | bytes 4194304 | tf_op jit(solution)/shard_map/all_to_all | solution.py:86
  405.1 5.2 %fusion.31 = bf16[256,32,128]{2,0,1:T(8,128)(2,1)} fusion(f32[128]{0:T(128)S(1)} %multiply_subtract_fusion.1, f32[256,32]{0,1:T(8,128)S(1)} %broadcast_add_fusion, bf16[256,32,128]{2,1,0:T(8,128)(2,1)S(1)} %bitcast.147, f32[256]{0:T(256)S(1)} %get-tuple-element.119, f32[256]{0:T(256)S(1)} %get-tuple-element.120), kind=kOutput, calls=%fused_computation.46 | convolution fusion | flops 1080557568 | bytes 4229632 | tf_op jit(solution)/shard_map/xyz,xk->kyz/dot_general | solution.py:96
  413.3 29.6 %all_to_all.74 = bf16[256,32,128]{2,1,0:T(8,128)(2,1)S(1)} all-to-all(bf16[256,32,128]{2,1,0:T(8,128)(2,1)S(1)} %copy.38), channel_id=1, replica_groups=mesh['box'=32,'pencil'=8] {'pencil'}, dimensions={0} | all-to-all | bytes 4194304 | tf_op jit(solution)/shard_map/all_to_all | solution.py:99
  443.5 4.2 convolution_bitcast_fusion
  (55 shorter events, 43.1 us)
Async XLA Ops:
  6.5 85.4 %all-gather.3.cloned.1.call-start = ((), (), s32[]{:S(2)}) async-start(), calls=%async_computation.4 | async-start | bytes 4325376 | tf_op jit(solution)/shard_map/all_gather | solution.py:62
  10.2 89.8 %copy-start.4 = (bf16[1,32,256,128]{3,2,1,0:T(8,128)(2,1)S(1)}, bf16[1,32,256,128]{3,2,1,0:T(8,128)(2,1)}, u32[]{:S(2)}) copy-start(bf16[1,32,256,128]{3,2,1,0:T(8,128)(2,1)} %param.21) | copy-start | bytes 6291460
  100.0 5.0 %copy-start.3 = (f32[32,256,128]{2,1,0:T(8,128)S(1)}, f32[32,256,128]{2,1,0:T(8,128)}, u32[]{:S(2)}) copy-start(f32[32,256,128]{2,1,0:T(8,128)} %bitcast_convert_fusion) | copy-start | bytes 12582916
  103.0 2.0 copy-start.1
  150.1 34.7 %all-to-all-start = ((bf16[32,256,128]{2,0,1:T(8,128)(2,1)}), bf16[32,256,128]{2,0,1:T(8,128)(2,1)}, u32[]{:S(2)}, u32[]{:S(2)}) async-start(bf16[32,256,128]{2,0,1:T(8,128)(2,1)} %copy.28), calls=%async_computation | async-start | bytes 4194304 | tf_op jit(solution)/shard_map/all_to_all | solution.py:86
  158.5 153.5 %all-gather.5.cloned.1.call-start = ((), (), s32[]{:S(2)}) async-start(), calls=%async_computation.5 | async-start | bytes 4325376 | tf_op jit(solution)/shard_map/all_gather | solution.py:62
  320.1 5.7 %copy-start.2 = (f32[32,256,128]{2,1,0:T(8,128)S(1)}, f32[32,256,128]{2,1,0:T(8,128)}, u32[]{:S(2)}) copy-start(f32[32,256,128]{2,1,0:T(8,128)} %get-tuple-element.115) | copy-start | bytes 12582916
  323.8 2.0 copy-start
Sparse Core Ops, SparseCore 0:
  9.9 81.9 all-gather.2
  238.5 73.5 all-gather.4
where the time goes:
time: 464 us; the launch traced here: 455 us
  waiting for transfers between devices  177 us (38%)
  blocking collectives  94.1 us (20%)
  local copies, waits for them, and re-layouts  89 us (19%)
  matrix products  36.3 us (8%)
  other arithmetic  36.1 us (8%)
  between operations  14 us (3%)
  starting transfers between devices  8.61 us (2%)
    all_gather x2, waiting for transfers between devices, shards(): gathered = lax.all_gather(export, 'box', axis=0, tiled=True)  151 us
    all_to_all x2, blocking collectives, shards(): lax.all_to_all(fifth_pass, 'pencil', split_axis=0, concat_axis=1, tiled=T...  59.4 us
    all_to_all x1, blocking collectives, shards(): lax.all_to_all(second_pass, 'pencil', split_axis=1, concat_axis=0, tiled=...  34.7 us
    scatter-add x2, local copies, waits for them, and re-layouts, shards(): boundary.at[:, :, depth_count - 1]  26 us
    all_to_all x1, waiting for transfers between devices, shards(): lax.all_to_all(second_pass, 'pencil', split_axis=1, concat_axis=0, tiled=...  25.9 us
    scatter-add x2, local copies, waits for them, and re-layouts, shards(): boundary = boundary.at[:, :, 0].add(REFLECT * iterate[:, :, 0])  21.9 us
    add x2, other arithmetic, shards(): boundary.at[:, :, depth_count - 1]  15.3 us
    dot_general x2, matrix products, shards(): jnp.einsum('xyz,yk->xkz', first_pass, width_table, preferred_element_type...  13.4 us
  transfers between devices with their start and end apart: 3, of which 3 were waited for; matrix products, arithmetic and copies ran while one was open for 1% of the time, Pallas kernels for 0%

commit v1 on v0

v1 whole, which is shorter than its diff:
```python
import functools

import jax
import jax.numpy as jnp
import ml_dtypes
import numpy as np
from jax import lax
from jax.experimental import pallas as pl
from jax.experimental.pallas import tpu as pltpu
from jax.sharding import PartitionSpec as P

W = 8
REFLECT = 0.6
TIMESTEP = 64.0
ZCHIPS = 8
SLAB = 16
CHUNK = 32
LOADS = 8

BF16 = ml_dtypes.bfloat16


def sine_table(length):
    ordinal = np.arange(length, dtype=np.float64) + 1.0
    phase_angle = np.pi * ordinal[:, None] * ordinal[None, :] / (length + 1.0)
    return np.sqrt(2.0 / (length + 1.0)) * np.sin(phase_angle)


def eigen_values(length):
    ordinal = np.arange(length, dtype=np.float64) + 1.0
    return 2.0 - 2.0 * np.cos(np.pi * ordinal / (length + 1.0))


def constants(planes, columns, heights):
    width = sine_table(columns)
    height = sine_table(heights).astype(BF16).astype(np.float64)
    gain = TIMESTEP * REFLECT
    faces = np.zeros((heights, heights))
    faces[0] = gain * height[0]
    faces[-1] = gain * height[-1]
    both = np.block([[height, height], [faces, np.zeros_like(faces)]])
    turn = gain * (np.outer(height[:, 0], height[0]) + np.outer(height[:, -1], height[-1]))
    nothing = np.zeros_like(turn)
    turns = np.block([[turn, nothing], [nothing, turn]])
    heights_two = np.block([[height, nothing], [nothing, height]])
    rows = np.concatenate([width[: W + 1], width[-W - 1 :]])
    rows = np.pad(rows, ((0, (-len(rows)) % 8), (0, 0)))
    slope = 2.0 + 1.0 / TIMESTEP + eigen_values(columns)[:, None] + eigen_values(heights)[None, :]
    ratio = 2.0 / (slope + np.sqrt(slope * slope - 4.0))
    weight = ratio / (1.0 - ratio * ratio) / TIMESTEP
    edge = np.broadcast_to(TIMESTEP * width[0][:, None], ratio.shape)
    modes = np.stack([ratio, planes * np.log(ratio), weight, edge])
    return dict(
        width=width.astype(BF16),
        height=height.astype(BF16),
        both=both.astype(BF16),
        turns=turns.astype(BF16),
        heights_two=heights_two.astype(BF16),
        rows=rows.astype(np.float32),
        modes=modes.astype(np.float32),
    )


def front_kernel(
    pencils, previous, source, neighbor, depth, wall, width, height, both, turns, rowtab, modes,
    out, prev, src, slab, right, force, carry, iterate, waves, inbox, own, gath0, gath1, packet, zbox0, zbox1,
    rows, ghost, walls, picks, load_sem, slab_sem, out_sem, x_send, x_recv, z_send, z_recv,
    w_send, w_recv,
):
    gath = (gath0, gath1)
    zbox = (zbox0, zbox1)
    planes, columns, heights = prev.shape
    pencil = lax.axis_index("pencil")
    box = lax.axis_index("box")
    boxes = neighbor.shape[0]
    xchips = boxes // ZCHIPS
    cx = box // ZCHIPS
    cz = box % ZCHIPS
    seglen = planes * pencils // neighbor.shape[2]
    segs = planes // seglen
    gain = TIMESTEP * REFLECT
    step = planes // LOADS

    x_peers = [(lax.rem(cx + k, xchips)) * ZCHIPS + cz for k in range(1, xchips)]
    z_peers = [cx * ZCHIPS + lax.rem(cz + k, ZCHIPS) for k in range(1, ZCHIPS)]
    w_peers = [lax.rem(pencil + k, pencils) for k in range(1, pencils)]

    barrier = pltpu.get_barrier_semaphore()
    for peer in x_peers + z_peers:
        pl.semaphore_signal(barrier, inc=1, device_id=(peer, pencil), device_id_type=pl.DeviceIdType.MESH)
    for peer in w_peers:
        pl.semaphore_signal(barrier, inc=1, device_id=(box, peer), device_id_type=pl.DeviceIdType.MESH)

    slab_loads = [
        pltpu.make_async_copy(previous.at[:, pl.ds(0, SLAB), :], slab.at[0], slab_sem.at[0]),
        pltpu.make_async_copy(previous.at[:, pl.ds(columns - SLAB, SLAB), :], slab.at[1], slab_sem.at[1]),
    ]
    for load in slab_loads:
        load.start()
    loads = []
    for c in range(LOADS):
        part = pl.ds(c * step, step)
        loads.append((
            pltpu.make_async_copy(previous.at[part], prev.at[part], load_sem.at[0, c]),
            pltpu.make_async_copy(source.at[part], src.at[part], load_sem.at[1, c]),
        ))
        loads[-1][0].start()
        loads[-1][1].start()

    lists = [(f, t) for f in range(2) for t in range(segs)]

    def search(b, found):
        return tuple(
            jnp.where(neighbor[b, f, pencil * segs + t] == box, depth[b, f, pencil * segs + t], d)
            for (f, t), d in zip(lists, found)
        )

    depths = lax.fori_loop(0, boxes, search, tuple(jnp.int32(1) for _ in lists))

    line = lax.broadcasted_iota(jnp.int32, (planes, heights), 0)
    for f in range(2):
        def mark(x, mask, f=f):
            return jnp.where(line == x, wall[f, x], mask)

        walls[f] = lax.fori_loop(0, planes, mark, jnp.zeros((planes, heights), jnp.int32))

    def x_copies(it):
        return [
            pltpu.make_async_remote_copy(
                gath[it].at[0], gath[it].at[k], x_send.at[it, k - 1], x_recv.at[it, k - 1],
                device_id=(x_peers[k - 1], pencil), device_id_type=pl.DeviceIdType.MESH,
            )
            for k in range(1, xchips)
        ]

    def z_copies(it):
        return [
            pltpu.make_async_remote_copy(
                packet.at[it, k - 1], zbox[it].at[k], z_send.at[it, k - 1], z_recv.at[it, k - 1],
                device_id=(z_peers[k - 1], pencil), device_id_type=pl.DeviceIdType.MESH,
            )
            for k in range(1, ZCHIPS)
        ]

    def w_copies(it):
        return [
            pltpu.make_async_remote_copy(
                waves.at[it, (pencil + k) // pencils], inbox.at[it, k - 1],
                w_send.at[it, k - 1], w_recv.at[it, k - 1],
                device_id=(box, w_peers[k - 1]), device_id_type=pl.DeviceIdType.MESH,
            )
            for k in range(1, pencils)
        ]

    def forward_margins(it):
        for k in range(ZCHIPS):
            reader = box if k == 0 else z_peers[k - 1]
            for j, (f, t) in enumerate(lists):
                donor = neighbor[reader, f, pencil * segs + t]
                block = gath[it][lax.rem(cx - donor // ZCHIPS + xchips, xchips), j]
                if k == 0:
                    zbox[it][0, j] = block
                else:
                    packet[it, k - 1, j] = block

    def imported(it, j):
        f, t = lists[j]
        donor = neighbor[box, f, pencil * segs + t]
        return zbox[it][lax.rem(cz - lax.rem(donor, ZCHIPS) + ZCHIPS, ZCHIPS), j].astype(jnp.float32)

    def imports(it, f):
        return jnp.concatenate([imported(it, f * segs + t) for t in range(segs)], axis=0)

    for load in slab_loads:
        load.wait()
    place = lax.broadcasted_iota(jnp.int32, (seglen, SLAB, heights), 1)
    for j, (f, t) in enumerate(lists):
        row = SLAB - 1 - depths[j] if f == 0 else depths[j]
        near = slab[1 - f, pl.ds(t * seglen, seglen)].astype(jnp.float32)
        gath0[0, j] = jnp.sum(jnp.where(place == row, near, 0.0), axis=1).astype(jnp.bfloat16)
    pl.semaphore_wait(barrier, len(x_peers) + len(z_peers) + len(w_peers))
    first_x = x_copies(0)
    for copy in first_x:
        copy.start()

    def transform(x, _):
        now = prev[x]
        total = (now.astype(jnp.float32) + src[x].astype(jnp.float32)).astype(jnp.bfloat16)
        turned = jnp.dot(
            width[...], jnp.concatenate([total, now], axis=1), preferred_element_type=jnp.float32
        ).astype(jnp.bfloat16)
        result = jnp.dot(turned, both[...], preferred_element_type=jnp.float32)
        right[x] = result[:, :heights]
        force[x] = result[:, heights:]
        return 0

    first_z = z_copies(0)
    for c in range(LOADS):
        for load in loads[c]:
            load.wait()
        lax.fori_loop(c * step, (c + 1) * step, transform, 0)
        if c == LOADS // 2 - 1:
            for copy in first_x:
                copy.wait_recv()
            forward_margins(0)
            for copy in first_z:
                copy.start()

    at_start = jnp.where(pencil == 0, gain, 0.0).astype(jnp.float32)
    at_end = jnp.where(pencil == pencils - 1, gain, 0.0).astype(jnp.float32)
    for x, scale in ((0, at_start), (planes - 1, at_end)):
        turned = jnp.dot(width[...], prev[x], preferred_element_type=jnp.float32).astype(jnp.bfloat16)
        right[x] += scale * jnp.dot(turned, height[...], preferred_element_type=jnp.float32)

    for copy in first_z:
        copy.wait_recv()
    for f in range(2):
        wallrow = slab[f, :, 0 if f == 0 else SLAB - 1, :].astype(jnp.float32)
        value = jnp.where(walls[f] == 1, REFLECT * wallrow, imports(0, f))
        ghost[f] = jnp.dot(value.astype(jnp.bfloat16), height[...], preferred_element_type=jnp.float32)

    parity = lax.broadcasted_iota(jnp.int32, (CHUNK, heights), 0) % 2
    sign = jnp.where(parity == 0, 1.0, -1.0).astype(jnp.float32)
    near_power = (2 * pencil + 1).astype(jnp.float32)
    far_power = (2 * pencils - 1 - 2 * pencil).astype(jnp.float32)

    def chunk_at(c):
        return pl.ds(pl.multiple_of(c * CHUNK, CHUNK), CHUNK)

    def sweep(it):
        def chunk(c, _):
            at = chunk_at(c)
            ratio = modes[0, at]
            edge = modes[3, at]

            def plane(i, carried):
                up, down, power = carried
                reach = ghost[0, pl.ds(i, 1), :] + sign * ghost[1, pl.ds(i, 1), :]
                value = right[i, at] + edge * reach
                right[i, at] = value
                return value + ratio * up, down + power * value, power * ratio

            zero = jnp.zeros((CHUNK, heights), jnp.float32)
            up, down, _ = lax.fori_loop(0, planes, plane, (zero, zero, zero + 1.0), unroll=4)
            log = modes[1, at]
            waves[it, 0, at] = (up - ratio * jnp.exp(log * near_power) * down).astype(jnp.bfloat16)
            waves[it, 1, at] = (down - ratio * jnp.exp(log * far_power) * up).astype(jnp.bfloat16)
            loop = ratio * ratio * jnp.exp(log * (2 * pencils - 1))
            own[0, at] = loop * up - ratio * jnp.exp(log * (near_power - 1.0)) * down
            own[1, at] = loop * down - ratio * jnp.exp(log * (far_power - 1.0)) * up
            return 0

        lax.fori_loop(0, columns // CHUNK, chunk, 0)

    def solve(it, done=None):
        def chunk(c, _):
            at = chunk_at(c)
            ratio = modes[0, at]
            log = modes[1, at]
            weight = modes[2, at]
            decay = jnp.exp(log)
            low = jnp.zeros((CHUNK, heights), jnp.float32)
            high = low
            for k in range(pencils - 1, 0, -1):
                here = jnp.where(pencil >= k, 1.0, 0.0).astype(jnp.float32)
                low = here * inbox[it, k - 1, at].astype(jnp.float32) + decay * low
            for k in range(1, pencils):
                here = jnp.where(pencil >= k, 0.0, 1.0).astype(jnp.float32)
                high = here * inbox[it, k - 1, at].astype(jnp.float32) + decay * high
            start = low + own[0, at] - ratio * jnp.exp(log * near_power) * high
            end = high + own[1, at] - ratio * jnp.exp(log * far_power) * low

            def rising(i, value):
                value = right[i, at] + ratio * value
                carry[i, at] = value
                return value

            lax.fori_loop(0, planes, rising, start, unroll=4)

            def falling(j, value):
                i = planes - 1 - j
                value = ratio * value
                iterate[i, at] = (weight * (carry[i, at] + value)).astype(jnp.bfloat16)
                return value + right[i, at]

            lax.fori_loop(0, planes, falling, end, unroll=4)
            if done is not None:
                done(c, at)
            return 0

        lax.fori_loop(0, columns // CHUNK, chunk, 0)

    sweep(0)
    first_w = w_copies(0)
    for copy in first_w:
        copy.start()
    for copy in first_w:
        copy.wait_recv()
    solve(0)

    picks[...] = jnp.zeros_like(picks)
    for t in range(segs):
        low_row = 2 * W + 1 - depths[t]
        high_row = depths[segs + t]
        for q, row in enumerate((0, 2 * W + 1, low_row, high_row)):
            picks[t, pl.ds(q, 1), :] = rowtab[pl.ds(row, 1), :]

    def pair_of(j):
        return jnp.concatenate([iterate[2 * j], iterate[2 * j + 1]], axis=1)

    for t in range(segs):
        lhs = picks[t].astype(jnp.bfloat16)

        def take(j, _):
            taken = jnp.dot(lhs, pair_of(j), preferred_element_type=jnp.float32)
            for q in range(4):
                rows[q, pl.ds(2 * j, 1), :] = taken[q : q + 1, :heights]
                rows[q, pl.ds(2 * j + 1, 1), :] = taken[q : q + 1, heights:]
            return 0

        lax.fori_loop(t * seglen // 2, (t + 1) * seglen // 2, take, 0)
    for j, (f, t) in enumerate(lists):
        gath1[0, j] = rows[2 + f, pl.ds(t * seglen, seglen), :].astype(jnp.bfloat16)
    second_x = x_copies(1)
    for copy in second_x:
        copy.start()

    def faces(j, _):
        added = jnp.dot(pair_of(j), turns[...], preferred_element_type=jnp.float32)
        right[2 * j] = force[2 * j] + added[:, :heights]
        right[2 * j + 1] = force[2 * j + 1] + added[:, heights:]
        return 0

    lax.fori_loop(0, planes // 4, faces, 0)
    for copy in second_x:
        copy.wait_recv()
    forward_margins(1)
    second_z = z_copies(1)
    for copy in second_z:
        copy.start()
    lax.fori_loop(planes // 4, planes // 2, faces, 0)
    right[0] += at_start * iterate[0].astype(jnp.float32)
    right[planes - 1] += at_end * iterate[planes - 1].astype(jnp.float32)
    for copy in second_z:
        copy.wait_recv()
    for f in range(2):
        ghost[f] = jnp.where(walls[f] == 1, REFLECT * rows[f], imports(1, f))

    sweep(1)
    second_w = w_copies(1)
    for copy in second_w:
        copy.start()
    for copy in second_w:
        copy.wait_recv()

    def store(c, at):
        pltpu.make_async_copy(iterate.at[:, at, :], out.at[:, at, :], out_sem.at[c]).start()

    solve(1, store)
    for c in range(columns // CHUNK):
        at = pl.ds(c * CHUNK, CHUNK)
        pltpu.make_async_copy(iterate.at[:, at, :], out.at[:, at, :], out_sem.at[c]).wait()
    for copy in first_x + first_z + first_w + second_x + second_z + second_w:
        copy.wait_send()


def back_kernel(modes, width, heights_two, solved):
    planes, _, heights = modes.shape
    for j in range(planes // 2):
        pair = jnp.concatenate([modes[2 * j], modes[2 * j + 1]], axis=1)
        half = jnp.dot(pair, heights_two[...], preferred_element_type=jnp.float32).astype(jnp.bfloat16)
        full = jnp.dot(width[...], half, preferred_element_type=jnp.float32)
        solved[2 * j] = full[:, :heights]
        solved[2 * j + 1] = full[:, heights:]


def shards(previous, source, neighbor, depth, wall):
    pencils = lax.axis_size("pencil")
    _, planes, columns, heights = previous.shape
    boxes, _, segments = neighbor.shape
    segs = planes * segments // (planes * pencils)
    seglen = planes // segs
    xchips = boxes // ZCHIPS
    table = {name: jnp.asarray(value) for name, value in constants(planes, columns, heights).items()}
    lists = 2 * segs
    field = (planes, columns, heights)
    block = (seglen, heights)
    vmem = pl.BlockSpec(memory_space=pltpu.VMEM)
    smem = pl.BlockSpec(memory_space=pltpu.SMEM)
    far = pl.BlockSpec(memory_space=pl.ANY)
    dma = pltpu.SemaphoreType.DMA
    modes = pl.pallas_call(
        functools.partial(front_kernel, pencils),
        out_shape=jax.ShapeDtypeStruct(field, jnp.bfloat16),
        in_specs=[far, far, smem, smem, smem] + [vmem] * 6,
        out_specs=far,
        scratch_shapes=[
            pltpu.VMEM(field, jnp.bfloat16),
            pltpu.VMEM(field, jnp.bfloat16),
            pltpu.VMEM((2, planes, SLAB, heights), jnp.bfloat16),
            pltpu.VMEM(field, jnp.float32),
            pltpu.VMEM(field, jnp.float32),
            pltpu.VMEM(field, jnp.float32),
            pltpu.VMEM(field, jnp.bfloat16),
            pltpu.VMEM((2, 2, columns, heights), jnp.bfloat16),
            pltpu.VMEM((2, pencils - 1, columns, heights), jnp.bfloat16),
            pltpu.VMEM((2, columns, heights), jnp.float32),
            pltpu.VMEM((xchips, lists) + block, jnp.bfloat16),
            pltpu.VMEM((xchips, lists) + block, jnp.bfloat16),
            pltpu.VMEM((2, ZCHIPS - 1, lists) + block, jnp.bfloat16),
            pltpu.VMEM((ZCHIPS, lists) + block, jnp.bfloat16),
            pltpu.VMEM((ZCHIPS, lists) + block, jnp.bfloat16),
            pltpu.VMEM((4, planes, heights), jnp.float32),
            pltpu.VMEM((2, planes, heights), jnp.float32),
            pltpu.VMEM((2, planes, heights), jnp.int32),
            pltpu.VMEM((segs, 8, columns), jnp.float32),
            dma((2, LOADS)),
            dma((2,)),
            dma((columns // CHUNK,)),
            dma((2, xchips - 1)),
            dma((2, xchips - 1)),
            dma((2, ZCHIPS - 1)),
            dma((2, ZCHIPS - 1)),
            dma((2, pencils - 1)),
            dma((2, pencils - 1)),
        ],
        compiler_params=pltpu.CompilerParams(
            collective_id=0, has_side_effects=True, vmem_limit_bytes=40 * 1024 * 1024
        ),
        name="schwarz_modes",
    )(
        previous[0], source[0], neighbor, depth, wall[0],
        table["width"], table["height"], table["both"], table["turns"], table["rows"], table["modes"],
    )
    group = 4
    solved = pl.pallas_call(
        back_kernel,
        out_shape=jax.ShapeDtypeStruct(field, jnp.float32),
        grid=(planes // group,),
        in_specs=[
            pl.BlockSpec((group, columns, heights), lambda i: (i, 0, 0)),
            pl.BlockSpec((columns, columns), lambda i: (0, 0)),
            pl.BlockSpec((2 * heights, 2 * heights), lambda i: (0, 0)),
        ],
        out_specs=pl.BlockSpec((group, columns, heights), lambda i: (i, 0, 0)),
        name="back_to_cells",
    )(modes, table["width"], table["heights_two"])
    return solved[None]


def solution(mesh):
    placed = (
        P("box", "pencil", None, None),
        P("box", "pencil", None, None),
        P(),
        P(),
        P("box", None, "pencil"),
    )
    return jax.shard_map(
        shards,
        mesh=mesh,
        in_specs=placed,
        out_specs=P("box", "pencil", None, None),
        check_vma=False,
    )
```

time: 464 us -> 79.4 us (0.17); the launches traced: 455 us -> 78.8 us
  waiting for transfers between devices: 177 us -> 0 us
  blocking collectives: 94.1 us -> 0 us
  local copies, waits for them, and re-layouts: 89 us -> 12 us
  Pallas kernels: 0 us -> 66.7 us
  matrix products: 36.3 us -> 0 us
  other arithmetic: 36.1 us -> 0 us
  between operations: 14 us -> 0.03 us
  starting transfers between devices: 8.61 us -> 0 us
    all_gather x2 -> x0, waiting for transfers between devices: 151 us -> none  [shards(): gathered = lax.all_gather(export, 'box', axis=0, tiled=True)]
    all_to_all x3 -> x0, blocking collectives: 94.1 us -> none  [the longest x2 59.4 us: shards(): lax.all_to_all(fifth_pass, 'pencil', split_axis=0, concat_axis=1, tiled=T...]
    pallas_call x0 -> x2, Pallas kernels: none -> 66.7 us  [the longest x1 58.9 us: shards(): pl.pallas_call(functools.partial(front_kernel, pencils), out_shape=jax.Sh...]
    scatter-add x8 -> x0, local copies, waits for them, and re-layouts: 56.1 us -> none  [the longest x2 26 us: shards(): boundary.at[:, :, depth_count - 1]]
    dot_general x6 -> x0, matrix products: 36.3 us -> none  [the longest x2 13.4 us: shards(): jnp.einsum('xyz,yk->xkz', first_pass, width_table, preferred_element_type...]
    add x9 -> x0, other arithmetic: 27.3 us -> none  [the longest x2 15.3 us: shards(): boundary.at[:, :, depth_count - 1]]
    all_to_all x1 -> x0, waiting for transfers between devices: 25.9 us -> none  [shards(): lax.all_to_all(second_pass, 'pencil', split_axis=1, concat_axis=0, tiled=...]
    convert_element_type x4 -> x0, local copies, waits for them, and re-layouts: 13.1 us -> none  [the longest x2 7.2 us: shards(): second_pass = jnp.einsum('xyz,yk->xkz', first_pass, width_table, preferre...]
  transfers between devices with their start and end apart: 3 -> 0, of which waited for: 3 -> 0; matrix products, arithmetic and copies ran while one was open for 1% -> 0% of each run, Pallas kernels for 0% -> 0%
where the time goes in v1:
time: 79.4 us; the launch traced here: 78.8 us
  Pallas kernels  66.7 us (84%)
  local copies, waits for them, and re-layouts  12 us (15%)
    pallas_call x1, Pallas kernels, shards(): pl.pallas_call(functools.partial(front_kernel, pencils), out_shape=jax.Sh...  58.9 us
    unnamed x22, local copies, waits for them, and re-layouts  12 us
    pallas_call x1, Pallas kernels, shards(): pl.pallas_call(back_kernel, out_shape=jax.ShapeDtypeStruct(field, jnp.flo...  7.8 us

profile of v1, /device:TPU:1, one launch (start us, length us, event | category | flops | bytes accessed | tf_op | source)
XLA Modules:
  0.0 78.8 jit_solution(10084946465450007685)
XLA Ops:
  0.0 0.8 %copy.13.neighbor = s32[32,2,16]{2,1,0:T(2,128)S(1)} copy(s32[32,2,16]{0,2,1:T(8,128)} %param.14) | data formatting | bytes 8192 | tf_op args[2]
  0.8 0.8 %copy.14.depth = s32[32,2,16]{2,1,0:T(2,128)S(1)} copy(s32[32,2,16]{0,2,1:T(8,128)} %param.15) | data formatting | bytes 8192 | tf_op args[3]
  1.6 0.0 copy-start.1
  1.6 1.6 %copy-done.1 = bf16[1,32,256,128]{3,2,1,0:T(8,128)(2,1)S(1)} copy-done((bf16[1,32,256,128]{3,2,1,0:T(8,128)(2,1)S(1)}, bf16[1,32,256,128]{3,2,1,0:T(8,128)(2,1)}, u32[]{:S(2)}) %copy-start.1) | copy-done | bytes 2097176
  3.2 0.0 copy-start.2
  3.2 1.6 %copy-done.2 = bf16[1,32,256,128]{3,2,1,0:T(8,128)(2,1)S(1)} copy-done((bf16[1,32,256,128]{3,2,1,0:T(8,128)(2,1)S(1)}, bf16[1,32,256,128]{3,2,1,0:T(8,128)(2,1)}, u32[]{:S(2)}) %copy-start.2) | copy-done | bytes 2097176
  4.8 0.0 copy-start.3
  4.8 0.9 %copy-done.3 = bf16[256,256]{1,0:T(8,128)(2,1)S(1)} copy-done((bf16[256,256]{1,0:T(8,128)(2,1)S(1)}, bf16[256,256]{1,0:T(8,128)(2,1)}, u32[]{:S(2)}) %copy-start.3) | copy-done | bytes 131096
  5.7 0.0 copy-start.4
  5.7 1.0 %copy-done.4 = f32[4,256,128]{2,1,0:T(8,128)S(1)} copy-done((f32[4,256,128]{2,1,0:T(8,128)S(1)}, f32[4,256,128]{2,1,0:T(8,128)}, u32[]{:S(2)}) %copy-start.4) | copy-done | bytes 524312
  6.7 0.0 copy-start.5
  6.7 0.9 %copy-done.5 = bf16[256,256]{1,0:T(8,128)(2,1)S(1)} copy-done((bf16[256,256]{1,0:T(8,128)(2,1)S(1)}, bf16[256,256]{1,0:T(8,128)(2,1)}, u32[]{:S(2)}) %copy-start.5) | copy-done | bytes 131096
  7.6 0.0 copy-start.6
  7.6 0.9 %copy-done.6 = bf16[256,256]{1,0:T(8,128)(2,1)S(1)} copy-done((bf16[256,256]{1,0:T(8,128)(2,1)S(1)}, bf16[256,256]{1,0:T(8,128)(2,1)}, u32[]{:S(2)}) %copy-start.6) | copy-done | bytes 131096
  8.5 0.0 copy-start.7
  8.5 0.8 copy-done.7
  9.3 0.0 copy-start.8
  9.3 0.7 copy-done.8
  10.0 0.0 copy-start.9
  10.0 0.7 copy-done.9
  10.7 58.9 %schwarz_modes.1.modes = bf16[32,256,128]{2,1,0:T(8,128)(2,1)S(1)} custom-call(bf16[32,256,128]{2,1,0:T(8,128)(2,1)S(1)} %bitcast.4, bf16[32,256,128]{2,1,0:T(8,128)(2,1)S(1)} %bitcast.5, s32[32,2,16]{2,1,0:T(2,128)S(1)} %copy.13.neighbor, s32[32,2,16]{2,1,0:T(2,128)S(1)} %copy.14.depth, s32[2,32]{1,0:T(2,128)S(1)} %bitcast.6, ...), custom_call_target="tpu_custom_call" | custom-call | tf_op jit(solution)/shard_map/schwarz_modes/pallas_call | solution.py:392
  69.7 0.0 copy-start
  69.7 1.3 %copy-done = bf16[32,256,128]{2,1,0:T(8,128)(2,1)} copy-done((bf16[32,256,128]{2,1,0:T(8,128)(2,1)}, bf16[32,256,128]{2,1,0:T(8,128)(2,1)S(1)}, u32[]{:S(2)}) %copy-start) | copy-done | bytes 2097176
  71.0 7.8 %back_to_cells.1 = f32[32,256,128]{2,1,0:T(8,128)} custom-call(bf16[32,256,128]{2,1,0:T(8,128)(2,1)} %copy-done, bf16[256,256]{1,0:T(8,128)(2,1)} %constant.14.clone.width, bf16[256,256]{1,0:T(8,128)(2,1)} %constant.18.clone.heights_two), custom_call_target="tpu_custom_call" | custom-call | tf_op jit(solution)/shard_map/back_to_cells/pallas_call | solution.py:436
Async XLA Ops:
  1.6 1.6 %copy-start.1 = (bf16[1,32,256,128]{3,2,1,0:T(8,128)(2,1)S(1)}, bf16[1,32,256,128]{3,2,1,0:T(8,128)(2,1)}, u32[]{:S(2)}) copy-start(bf16[1,32,256,128]{3,2,1,0:T(8,128)(2,1)} %param.12) | copy-start | bytes 6291460
  3.2 1.6 %copy-start.2 = (bf16[1,32,256,128]{3,2,1,0:T(8,128)(2,1)S(1)}, bf16[1,32,256,128]{3,2,1,0:T(8,128)(2,1)}, u32[]{:S(2)}) copy-start(bf16[1,32,256,128]{3,2,1,0:T(8,128)(2,1)} %param.13) | copy-start | bytes 6291460
  4.8 0.9 %copy-start.3 = (bf16[256,256]{1,0:T(8,128)(2,1)S(1)}, bf16[256,256]{1,0:T(8,128)(2,1)}, u32[]{:S(2)}) copy-start(bf16[256,256]{1,0:T(8,128)(2,1)} %constant.14.clone.width) | copy-start | bytes 393220
  5.7 1.0 %copy-start.4 = (f32[4,256,128]{2,1,0:T(8,128)S(1)}, f32[4,256,128]{2,1,0:T(8,128)}, u32[]{:S(2)}) copy-start(f32[4,256,128]{2,1,0:T(8,128)} %constant.20.clone.modes) | copy-start | bytes 1572868
  6.7 0.9 %copy-start.5 = (bf16[256,256]{1,0:T(8,128)(2,1)S(1)}, bf16[256,256]{1,0:T(8,128)(2,1)}, u32[]{:S(2)}) copy-start(bf16[256,256]{1,0:T(8,128)(2,1)} %constant.17.clone.turns) | copy-start | bytes 393220
  7.6 0.9 %copy-start.6 = (bf16[256,256]{1,0:T(8,128)(2,1)S(1)}, bf16[256,256]{1,0:T(8,128)(2,1)}, u32[]{:S(2)}) copy-start(bf16[256,256]{1,0:T(8,128)(2,1)} %constant.16.clone.both) | copy-start | bytes 393220
  8.5 0.8 copy-start.7
  9.3 0.7 copy-start.8
  10.0 0.7 copy-start.9
  69.7 1.3 %copy-start = (bf16[32,256,128]{2,1,0:T(8,128)(2,1)}, bf16[32,256,128]{2,1,0:T(8,128)(2,1)S(1)}, u32[]{:S(2)}) copy-start(bf16[32,256,128]{2,1,0:T(8,128)(2,1)S(1)} %schwarz_modes.1.modes) | copy-start | bytes 6291460

commit v2 on v1

--- a/solution.py
+++ b/solution.py
@@ -62,9 +62,22 @@
 
 
 def front_kernel(
-    pencils, previous, source, neighbor, depth, wall, width, height, both, turns, rowtab, modes,
+    pencils, previous, source, neighbor_far, depth_far, wall_far, *more
+):
+    tables_far, (out, neighbor, depth, wall), more = more[:6], more[6:10], more[10:]
+    tables, more = more[:6], more[6:]
+    width, height, both, turns, rowtab, modes = tables
+    run_front(
+        pencils, previous, source, (neighbor_far, depth_far, wall_far) + tables_far,
+        (neighbor, depth, wall) + tables, *tables, neighbor, depth, wall, out, *more
+    )
+
+
+def run_front(
+    pencils, previous, source, smalls_far, smalls, width, height, both, turns, rowtab, modes,
+    neighbor, depth, wall,
     out, prev, src, slab, right, force, carry, iterate, waves, inbox, own, gath0, gath1, packet, zbox0, zbox1,
-    rows, ghost, walls, picks, load_sem, slab_sem, out_sem, x_send, x_recv, z_send, z_recv,
+    rows, ghost, walls, picks, load_sem, slab_sem, small_sem, out_sem, x_send, x_recv, z_send, z_recv,
     w_send, w_recv,
 ):
     gath = (gath0, gath1)
@@ -72,11 +85,11 @@
     planes, columns, heights = prev.shape
     pencil = lax.axis_index("pencil")
     box = lax.axis_index("box")
-    boxes = neighbor.shape[0]
+    boxes = neighbor.shape[2]
     xchips = boxes // ZCHIPS
     cx = box // ZCHIPS
     cz = box % ZCHIPS
-    seglen = planes * pencils // neighbor.shape[2]
+    seglen = planes * pencils // neighbor.shape[1]
     segs = planes // seglen
     gain = TIMESTEP * REFLECT
     step = planes // LOADS
@@ -95,7 +108,11 @@
         pltpu.make_async_copy(previous.at[:, pl.ds(0, SLAB), :], slab.at[0], slab_sem.at[0]),
         pltpu.make_async_copy(previous.at[:, pl.ds(columns - SLAB, SLAB), :], slab.at[1], slab_sem.at[1]),
     ]
-    for load in slab_loads:
+    small_loads = [
+        pltpu.make_async_copy(there, here, small_sem.at[i])
+        for i, (there, here) in enumerate(zip(smalls_far, smalls))
+    ]
+    for load in slab_loads + small_loads:
         load.start()
     loads = []
     for c in range(LOADS):
@@ -107,11 +124,13 @@
         loads[-1][0].start()
         loads[-1][1].start()
 
+    for load in small_loads:
+        load.wait()
     lists = [(f, t) for f in range(2) for t in range(segs)]
 
     def search(b, found):
         return tuple(
-            jnp.where(neighbor[b, f, pencil * segs + t] == box, depth[b, f, pencil * segs + t], d)
+            jnp.where(neighbor[f, pencil * segs + t, b] == box, depth[f, pencil * segs + t, b], d)
             for (f, t), d in zip(lists, found)
         )
 
@@ -156,7 +175,7 @@
         for k in range(ZCHIPS):
             reader = box if k == 0 else z_peers[k - 1]
             for j, (f, t) in enumerate(lists):
-                donor = neighbor[reader, f, pencil * segs + t]
+                donor = neighbor[f, pencil * segs + t, reader]
                 block = gath[it][lax.rem(cx - donor // ZCHIPS + xchips, xchips), j]
                 if k == 0:
                     zbox[it][0, j] = block
@@ -165,7 +184,7 @@
 
     def imported(it, j):
         f, t = lists[j]
-        donor = neighbor[box, f, pencil * segs + t]
+        donor = neighbor[f, pencil * segs + t, box]
         return zbox[it][lax.rem(cz - lax.rem(donor, ZCHIPS) + ZCHIPS, ZCHIPS), j].astype(jnp.float32)
 
     def imports(it, f):
@@ -385,16 +404,21 @@
     lists = 2 * segs
     field = (planes, columns, heights)
     block = (seglen, heights)
-    vmem = pl.BlockSpec(memory_space=pltpu.VMEM)
-    smem = pl.BlockSpec(memory_space=pltpu.SMEM)
-    far = pl.BlockSpec(memory_space=pl.ANY)
+    far = pl.BlockSpec(memory_space=pltpu.HBM)
+    names = ("width", "height", "both", "turns", "rows", "modes")
     dma = pltpu.SemaphoreType.DMA
     modes = pl.pallas_call(
         functools.partial(front_kernel, pencils),
         out_shape=jax.ShapeDtypeStruct(field, jnp.bfloat16),
-        in_specs=[far, far, smem, smem, smem] + [vmem] * 6,
+        in_specs=[far] * (5 + len(names)),
         out_specs=far,
         scratch_shapes=[
+            pltpu.SMEM((2, segments, boxes), jnp.int32),
+            pltpu.SMEM((2, segments, boxes), jnp.int32),
+            pltpu.SMEM((2, planes), jnp.int32),
+        ]
+        + [pltpu.VMEM(table[name].shape, table[name].dtype) for name in names]
+        + [
             pltpu.VMEM(field, jnp.bfloat16),
             pltpu.VMEM(field, jnp.bfloat16),
             pltpu.VMEM((2, planes, SLAB, heights), jnp.bfloat16),
@@ -416,6 +440,7 @@
             pltpu.VMEM((segs, 8, columns), jnp.float32),
             dma((2, LOADS)),
             dma((2,)),
+            dma((3 + len(names),)),
             dma((columns // CHUNK,)),
             dma((2, xchips - 1)),
             dma((2, xchips - 1)),
@@ -425,14 +450,14 @@
             dma((2, pencils - 1)),
         ],
         compiler_params=pltpu.CompilerParams(
-            collective_id=0, has_side_effects=True, vmem_limit_bytes=40 * 1024 * 1024
+            collective_id=0, has_side_effects=True, vmem_limit_bytes=67_043_328
         ),
         name="schwarz_modes",
     )(
-        previous[0], source[0], neighbor, depth, wall[0],
-        table["width"], table["height"], table["both"], table["turns"], table["rows"], table["modes"],
+        previous[0], source[0], neighbor.transpose(1, 2, 0), depth.transpose(1, 2, 0), wall[0],
+        *[table[name] for name in names],
     )
-    group = 4
+    group = 8
     solved = pl.pallas_call(
         back_kernel,
         out_shape=jax.ShapeDtypeStruct(field, jnp.float32),

time: 79.4 us -> 63.9 us (0.80)
  local copies, waits for them, and re-layouts: 12 us -> 0 us
  Pallas kernels: 66.7 us -> 63.8 us
    unnamed x22 -> x0, local copies, waits for them, and re-layouts: 12 us -> none
    pallas_call x1, Pallas kernels: 7.8 us -> 5.38 us  [shards(): pl.pallas_call(back_kernel, out_shape=jax.ShapeDtypeStruct(field, jnp.flo...]
where the time goes in v2:
time: 63.9 us; the launch traced here: 63.8 us
  Pallas kernels  63.8 us (100%)
    pallas_call x1, Pallas kernels, shards(): pl.pallas_call(functools.partial(front_kernel, pencils), out_shape=jax.Sh...  58.4 us
    pallas_call x1, Pallas kernels, shards(): pl.pallas_call(back_kernel, out_shape=jax.ShapeDtypeStruct(field, jnp.flo...  5.38 us

profile of v2, /device:TPU:1, one launch (start us, length us, event | category | flops | bytes accessed | tf_op | source)
XLA Modules:
  0.0 63.8 jit_solution(10166099344689473176)
XLA Ops:
  0.0 58.4 %schwarz_modes.1.modes = bf16[32,256,128]{2,1,0:T(8,128)(2,1)} custom-call(bf16[32,256,128]{2,1,0:T(8,128)(2,1)} %bitcast.6, bf16[32,256,128]{2,1,0:T(8,128)(2,1)} %bitcast.7, s32[2,16,32]{2,1,0:T(8,128)} %bitcast.8, s32[2,16,32]{2,1,0:T(8,128)} %bitcast.9, s32[2,32]{1,0:T(2,128)} %bitcast.10, bf16[256,256]{1,0:T(8,128)(2,1)} %constant.14.clone.more_0_.width, ...), custom_call_target="tpu_custom_call" | custom-call | tf_op jit(solution)/shard_map/schwarz_modes/pallas_call | solution.py:410
  58.4 5.4 %back_to_cells.1 = f32[32,256,128]{2,1,0:T(8,128)} custom-call(bf16[32,256,128]{2,1,0:T(8,128)(2,1)} %schwarz_modes.1.modes, bf16[256,256]{1,0:T(8,128)(2,1)} %constant.14.clone.more_0_.width, bf16[256,256]{1,0:T(8,128)(2,1)} %constant.18.clone.heights_two), custom_call_target="tpu_custom_call" | custom-call | tf_op jit(solution)/shard_map/back_to_cells/pallas_call | solution.py:461

commit v3 on v2

--- a/solution.py
+++ b/solution.py
@@ -14,8 +14,8 @@
 TIMESTEP = 64.0
 ZCHIPS = 8
 SLAB = 16
-CHUNK = 32
-LOADS = 8
+CHUNK = 64
+LOADS = 4
 
 BF16 = ml_dtypes.bfloat16
 
@@ -45,6 +45,7 @@
     heights_two = np.block([[height, nothing], [nothing, height]])
     rows = np.concatenate([width[: W + 1], width[-W - 1 :]])
     rows = np.pad(rows, ((0, (-len(rows)) % 8), (0, 0)))
+    rows = rows.reshape(len(rows), columns // CHUNK, CHUNK).transpose(1, 0, 2)
     slope = 2.0 + 1.0 / TIMESTEP + eigen_values(columns)[:, None] + eigen_values(heights)[None, :]
     ratio = 2.0 / (slope + np.sqrt(slope * slope - 4.0))
     weight = ratio / (1.0 - ratio * ratio) / TIMESTEP
@@ -64,9 +65,8 @@
 def front_kernel(
     pencils, previous, source, neighbor_far, depth_far, wall_far, *more
 ):
-    tables_far, (out, neighbor, depth, wall), more = more[:6], more[6:10], more[10:]
-    tables, more = more[:6], more[6:]
-    width, height, both, turns, rowtab, modes = tables
+    tables_far, (out, neighbor, depth, wall), more = more[:7], more[7:11], more[11:]
+    tables, more = more[:7], more[7:]
     run_front(
         pencils, previous, source, (neighbor_far, depth_far, wall_far) + tables_far,
         (neighbor, depth, wall) + tables, *tables, neighbor, depth, wall, out, *more
@@ -74,7 +74,7 @@
 
 
 def run_front(
-    pencils, previous, source, smalls_far, smalls, width, height, both, turns, rowtab, modes,
+    pencils, previous, source, smalls_far, smalls, width, height, both, turns, heights_two, rowtab, modes,
     neighbor, depth, wall,
     out, prev, src, slab, right, force, carry, iterate, waves, inbox, own, gath0, gath1, packet, zbox0, zbox1,
     rows, ghost, walls, picks, load_sem, slab_sem, small_sem, out_sem, x_send, x_recv, z_send, z_recv,
@@ -93,6 +93,7 @@
     segs = planes // seglen
     gain = TIMESTEP * REFLECT
     step = planes // LOADS
+    half = planes // 2
 
     x_peers = [(lax.rem(cx + k, xchips)) * ZCHIPS + cz for k in range(1, xchips)]
     z_peers = [cx * ZCHIPS + lax.rem(cz + k, ZCHIPS) for k in range(1, ZCHIPS)]
@@ -114,15 +115,17 @@
     ]
     for load in slab_loads + small_loads:
         load.start()
-    loads = []
-    for c in range(LOADS):
+
+    def field_loads(c):
         part = pl.ds(c * step, step)
-        loads.append((
+        return (
             pltpu.make_async_copy(previous.at[part], prev.at[part], load_sem.at[0, c]),
             pltpu.make_async_copy(source.at[part], src.at[part], load_sem.at[1, c]),
-        ))
-        loads[-1][0].start()
-        loads[-1][1].start()
+        )
+
+    for c in range(LOADS):
+        for load in field_loads(c):
+            load.start()
 
     for load in small_loads:
         load.wait()
@@ -142,6 +145,11 @@
             return jnp.where(line == x, wall[f, x], mask)
 
         walls[f] = lax.fori_loop(0, planes, mark, jnp.zeros((planes, heights), jnp.int32))
+
+    chunks = columns // CHUNK
+
+    def chunk_at(c):
+        return pl.ds(c * CHUNK, CHUNK)
 
     def x_copies(it):
         return [
@@ -161,11 +169,12 @@
             for k in range(1, ZCHIPS)
         ]
 
-    def w_copies(it):
+    def w_copies(it, c):
+        at = chunk_at(c)
         return [
             pltpu.make_async_remote_copy(
-                waves.at[it, (pencil + k) // pencils], inbox.at[it, k - 1],
-                w_send.at[it, k - 1], w_recv.at[it, k - 1],
+                waves.at[it, (pencil + k) // pencils, at], inbox.at[it, k - 1, at],
+                w_send.at[it, c, k - 1], w_recv.at[it, c, k - 1],
                 device_id=(box, w_peers[k - 1]), device_id_type=pl.DeviceIdType.MESH,
             )
             for k in range(1, pencils)
@@ -215,9 +224,9 @@
 
     first_z = z_copies(0)
     for c in range(LOADS):
-        for load in loads[c]:
+        for load in field_loads(c):
             load.wait()
-        lax.fori_loop(c * step, (c + 1) * step, transform, 0)
+        lax.fori_loop(c * step, (c + 1) * step, transform, 0, unroll=4)
         if c == LOADS // 2 - 1:
             for copy in first_x:
                 copy.wait_recv()
@@ -243,11 +252,8 @@
     near_power = (2 * pencil + 1).astype(jnp.float32)
     far_power = (2 * pencils - 1 - 2 * pencil).astype(jnp.float32)
 
-    def chunk_at(c):
-        return pl.ds(pl.multiple_of(c * CHUNK, CHUNK), CHUNK)
-
     def sweep(it):
-        def chunk(c, _):
+        def chunk(c):
             at = chunk_at(c)
             ratio = modes[0, at]
             edge = modes[3, at]
@@ -267,13 +273,17 @@
             loop = ratio * ratio * jnp.exp(log * (2 * pencils - 1))
             own[0, at] = loop * up - ratio * jnp.exp(log * (near_power - 1.0)) * down
             own[1, at] = loop * down - ratio * jnp.exp(log * (far_power - 1.0)) * up
-            return 0
-
-        lax.fori_loop(0, columns // CHUNK, chunk, 0)
-
-    def solve(it, done=None):
-        def chunk(c, _):
+            for copy in w_copies(it, c):
+                copy.start()
+
+        for c in range(chunks):
+            chunk(c)
+
+    def solve(it, done):
+        def chunk(c):
             at = chunk_at(c)
+            for copy in w_copies(it, c):
+                copy.wait_recv()
             ratio = modes[0, at]
             log = modes[1, at]
             weight = modes[2, at]
@@ -289,108 +299,136 @@
             start = low + own[0, at] - ratio * jnp.exp(log * near_power) * high
             end = high + own[1, at] - ratio * jnp.exp(log * far_power) * low
 
-            def rising(i, value):
-                value = right[i, at] + ratio * value
-                carry[i, at] = value
-                return value
-
-            lax.fori_loop(0, planes, rising, start, unroll=4)
-
-            def falling(j, value):
-                i = planes - 1 - j
-                value = ratio * value
-                iterate[i, at] = (weight * (carry[i, at] + value)).astype(jnp.bfloat16)
-                return value + right[i, at]
-
-            lax.fori_loop(0, planes, falling, end, unroll=4)
-            if done is not None:
-                done(c, at)
-            return 0
-
-        lax.fori_loop(0, columns // CHUNK, chunk, 0)
+            def outer(j, carried):
+                up, down = carried
+                i, m = j, planes - 1 - j
+                up = right[i, at] + ratio * up
+                down = ratio * down
+                carry[i, at] = up
+                carry[m, at] = down
+                return up, down + right[m, at]
+
+            def inner(j, carried):
+                up, down = carried
+                i, m = j, planes - 1 - j
+                up = right[i, at] + ratio * up
+                down = ratio * down
+                iterate[i, at] = (weight * (carry[i, at] + up)).astype(jnp.bfloat16)
+                iterate[m, at] = (weight * (carry[m, at] + down)).astype(jnp.bfloat16)
+                return up, down + right[m, at]
+
+            carried = lax.fori_loop(0, half, outer, (start, end), unroll=4)
+            lax.fori_loop(half, planes, inner, carried, unroll=4)
+            done(c, at)
+
+        for c in range(chunks):
+            chunk(c)
 
     sweep(0)
-    first_w = w_copies(0)
-    for copy in first_w:
-        copy.start()
-    for copy in first_w:
-        copy.wait_recv()
-    solve(0)
 
     picks[...] = jnp.zeros_like(picks)
+    wanted = [0, 2 * W + 1]
     for t in range(segs):
-        low_row = 2 * W + 1 - depths[t]
-        high_row = depths[segs + t]
-        for q, row in enumerate((0, 2 * W + 1, low_row, high_row)):
-            picks[t, pl.ds(q, 1), :] = rowtab[pl.ds(row, 1), :]
-
-    def pair_of(j):
-        return jnp.concatenate([iterate[2 * j], iterate[2 * j + 1]], axis=1)
-
-    for t in range(segs):
-        lhs = picks[t].astype(jnp.bfloat16)
-
-        def take(j, _):
-            taken = jnp.dot(lhs, pair_of(j), preferred_element_type=jnp.float32)
-            for q in range(4):
-                rows[q, pl.ds(2 * j, 1), :] = taken[q : q + 1, :heights]
-                rows[q, pl.ds(2 * j + 1, 1), :] = taken[q : q + 1, heights:]
-            return 0
-
-        lax.fori_loop(t * seglen // 2, (t + 1) * seglen // 2, take, 0)
+        wanted += [2 * W + 1 - depths[t], depths[segs + t]]
+    for c in range(chunks):
+        for q, row in enumerate(wanted):
+            picks[c, pl.ds(q, 1), :] = rowtab[c, pl.ds(row, 1), :]
+    rows[...] = jnp.zeros_like(rows)
+
+    def pair_of(j, at=slice(None)):
+        return jnp.concatenate([iterate[j, at], iterate[half + j, at]], axis=1)
+
+    def take(c, at):
+        lhs = picks[c].astype(jnp.bfloat16)
+        for j in range(half):
+            rows[j] += jnp.dot(lhs, pair_of(j, at), preferred_element_type=jnp.float32)
+
+    solve(0, take)
+
+    def row_at(q, t):
+        return rows[:, q, t * heights : (t + 1) * heights]
+
     for j, (f, t) in enumerate(lists):
-        gath1[0, j] = rows[2 + f, pl.ds(t * seglen, seglen), :].astype(jnp.bfloat16)
+        gath1[0, j] = row_at(2 + 2 * t + f, t).astype(jnp.bfloat16)
     second_x = x_copies(1)
     for copy in second_x:
         copy.start()
 
     def faces(j, _):
         added = jnp.dot(pair_of(j), turns[...], preferred_element_type=jnp.float32)
-        right[2 * j] = force[2 * j] + added[:, :heights]
-        right[2 * j + 1] = force[2 * j + 1] + added[:, heights:]
+        right[j] = force[j] + added[:, :heights]
+        right[half + j] = force[half + j] + added[:, heights:]
         return 0
 
-    lax.fori_loop(0, planes // 4, faces, 0)
+    lax.fori_loop(0, half // 2, faces, 0, unroll=4)
     for copy in second_x:
         copy.wait_recv()
     forward_margins(1)
     second_z = z_copies(1)
     for copy in second_z:
         copy.start()
-    lax.fori_loop(planes // 4, planes // 2, faces, 0)
+    lax.fori_loop(half // 2, half, faces, 0, unroll=4)
     right[0] += at_start * iterate[0].astype(jnp.float32)
     right[planes - 1] += at_end * iterate[planes - 1].astype(jnp.float32)
     for copy in second_z:
         copy.wait_recv()
     for f in range(2):
-        ghost[f] = jnp.where(walls[f] == 1, REFLECT * rows[f], imports(1, f))
+        wallrows = jnp.concatenate([row_at(f, t) for t in range(segs)], axis=0)
+        ghost[f] = jnp.where(walls[f] == 1, REFLECT * wallrows, imports(1, f))
 
     sweep(1)
-    second_w = w_copies(1)
-    for copy in second_w:
-        copy.start()
-    for copy in second_w:
-        copy.wait_recv()
-
-    def store(c, at):
-        pltpu.make_async_copy(iterate.at[:, at, :], out.at[:, at, :], out_sem.at[c]).start()
-
-    solve(1, store)
-    for c in range(columns // CHUNK):
-        at = pl.ds(c * CHUNK, CHUNK)
-        pltpu.make_async_copy(iterate.at[:, at, :], out.at[:, at, :], out_sem.at[c]).wait()
-    for copy in first_x + first_z + first_w + second_x + second_z + second_w:
+
+    def to_cells(c, at):
+        for j in range(half):
+            cells = jnp.dot(pair_of(j, at), heights_two[...], preferred_element_type=jnp.float32)
+            src[j, at] = cells[:, :heights].astype(jnp.bfloat16)
+            src[half + j, at] = cells[:, heights:].astype(jnp.bfloat16)
+        pltpu.make_async_copy(src.at[:, at, :], out.at[:, at, :], out_sem.at[c]).start()
+
+    solve(1, to_cells)
+
+    for c in range(chunks):
+        at = chunk_at(c)
+        pltpu.make_async_copy(src.at[:, at, :], out.at[:, at, :], out_sem.at[c]).wait()
+        for it in range(2):
+            for copy in w_copies(it, c):
+                copy.wait_send()
+    for copy in first_x + first_z + second_x + second_z:
         copy.wait_send()
 
 
-def back_kernel(modes, width, heights_two, solved):
-    planes, _, heights = modes.shape
-    for j in range(planes // 2):
-        pair = jnp.concatenate([modes[2 * j], modes[2 * j + 1]], axis=1)
-        half = jnp.dot(pair, heights_two[...], preferred_element_type=jnp.float32).astype(jnp.bfloat16)
-        full = jnp.dot(width[...], half, preferred_element_type=jnp.float32)
-        solved[2 * j] = full[:, :heights]
-        solved[2 * j + 1] = full[:, heights:]
+def back_kernel(turned_far, width_far, solved_far, turned, width, solved, load_sem, width_sem, store_sem):
+    planes, _, heights = turned.shape
+    step = planes // LOADS
+
+    def load(c):
+        part = pl.ds(c * step, step)
+        return pltpu.make_async_copy(turned_far.at[part], turned.at[part], load_sem.at[c])
+
+    def store(c):
+        part = pl.ds(c * step, step)
+        return pltpu.make_async_copy(solved.at[part], solved_far.at[part], store_sem.at[c])
+
+    table = pltpu.make_async_copy(width_far, width, width_sem)
+    table.start()
+    for c in range(LOADS):
+        load(c).start()
+    table.wait()
+
+    def piece(c, _):
+        load(c).wait()
+        for j in range(0, step, 2):
+            x = c * step + j
+            pair = jnp.concatenate([turned[x], turned[x + 1]], axis=1)
+            full = jnp.dot(width[...], pair, preferred_element_type=jnp.float32)
+            solved[x] = full[:, :heights]
+            solved[x + 1] = full[:, heights:]
+        store(c).start()
+        return 0
+
+    lax.fori_loop(0, LOADS, piece, 0)
+    for c in range(LOADS):
+        store(c).wait()
 
 
 def shards(previous, source, neighbor, depth, wall):
@@ -405,9 +443,9 @@
     field = (planes, columns, heights)
     block = (seglen, heights)
     far = pl.BlockSpec(memory_space=pltpu.HBM)
-    names = ("width", "height", "both", "turns", "rows", "modes")
+    names = ("width", "height", "both", "turns", "heights_two", "rows", "modes")
     dma = pltpu.SemaphoreType.DMA
-    modes = pl.pallas_call(
+    turned = pl.pallas_call(
         functools.partial(front_kernel, pencils),
         out_shape=jax.ShapeDtypeStruct(field, jnp.bfloat16),
         in_specs=[far] * (5 + len(names)),
@@ -434,10 +472,10 @@
             pltpu.VMEM((2, ZCHIPS - 1, lists) + block, jnp.bfloat16),
             pltpu.VMEM((ZCHIPS, lists) + block, jnp.bfloat16),
             pltpu.VMEM((ZCHIPS, lists) + block, jnp.bfloat16),
-            pltpu.VMEM((4, planes, heights), jnp.float32),
+            pltpu.VMEM((planes // 2, 8, 2 * heights), jnp.float32),
             pltpu.VMEM((2, planes, heights), jnp.float32),
             pltpu.VMEM((2, planes, heights), jnp.int32),
-            pltpu.VMEM((segs, 8, columns), jnp.float32),
+            pltpu.VMEM((columns // CHUNK, 8, CHUNK), jnp.float32),
             dma((2, LOADS)),
             dma((2,)),
             dma((3 + len(names),)),
@@ -446,8 +484,8 @@
             dma((2, xchips - 1)),
             dma((2, ZCHIPS - 1)),
             dma((2, ZCHIPS - 1)),
-            dma((2, pencils - 1)),
-            dma((2, pencils - 1)),
+            dma((2, columns // CHUNK, pencils - 1)),
+            dma((2, columns // CHUNK, pencils - 1)),
         ],
         compiler_params=pltpu.CompilerParams(
             collective_id=0, has_side_effects=True, vmem_limit_bytes=67_043_328
@@ -457,19 +495,22 @@
         previous[0], source[0], neighbor.transpose(1, 2, 0), depth.transpose(1, 2, 0), wall[0],
         *[table[name] for name in names],
     )
-    group = 8
     solved = pl.pallas_call(
         back_kernel,
         out_shape=jax.ShapeDtypeStruct(field, jnp.float32),
-        grid=(planes // group,),
-        in_specs=[
-            pl.BlockSpec((group, columns, heights), lambda i: (i, 0, 0)),
-            pl.BlockSpec((columns, columns), lambda i: (0, 0)),
-            pl.BlockSpec((2 * heights, 2 * heights), lambda i: (0, 0)),
+        in_specs=[far, far],
+        out_specs=far,
+        scratch_shapes=[
+            pltpu.VMEM(field, jnp.bfloat16),
+            pltpu.VMEM((columns, columns), jnp.bfloat16),
+            pltpu.VMEM(field, jnp.float32),
+            dma((LOADS,)),
+            dma(()),
+            dma((LOADS,)),
         ],
-        out_specs=pl.BlockSpec((group, columns, heights), lambda i: (i, 0, 0)),
+        compiler_params=pltpu.CompilerParams(vmem_limit_bytes=67_043_328),
         name="back_to_cells",
-    )(modes, table["width"], table["heights_two"])
+    )(turned, table["width"])
     return solved[None]
 
 

time: 63.9 us -> 50.5 us (0.79)
  Pallas kernels: 63.8 us -> 50.4 us
    pallas_call x1, Pallas kernels: 58.4 us -> 46.6 us  [shards(): pl.pallas_call(functools.partial(front_kernel, pencils), out_shape=jax.Sh...]
    pallas_call x1, Pallas kernels: 5.38 us -> 3.77 us  [shards(): pl.pallas_call(back_kernel, out_shape=jax.ShapeDtypeStruct(field, jnp.flo...]
where the time goes in v3:
time: 50.5 us; the launch traced here: 50.4 us
  Pallas kernels  50.4 us (100%)
    pallas_call x1, Pallas kernels, shards(): pl.pallas_call(functools.partial(front_kernel, pencils), out_shape=jax.Sh...  46.6 us
    pallas_call x1, Pallas kernels, shards(): pl.pallas_call(back_kernel, out_shape=jax.ShapeDtypeStruct(field, jnp.flo...  3.77 us

profile of v3, /device:TPU:1, one launch (start us, length us, event | category | flops | bytes accessed | tf_op | source)
XLA Modules:
  0.0 50.4 jit_solution(7694640584074667862)
XLA Ops:
  0.0 46.6 %schwarz_modes.1.turned_far = bf16[32,256,128]{2,1,0:T(8,128)(2,1)} custom-call(bf16[32,256,128]{2,1,0:T(8,128)(2,1)} %bitcast.6, bf16[32,256,128]{2,1,0:T(8,128)(2,1)} %bitcast.7, s32[2,16,32]{2,1,0:T(8,128)} %bitcast.8, s32[2,16,32]{2,1,0:T(8,128)} %bitcast.9, s32[2,32]{1,0:T(2,128)} %bitcast.10, bf16[256,256]{1,0:T(8,128)(2,1)} %constant.14.clone.more_0_.width_far, ...), custom_call_target="tpu_custom_call" | custom-call | tf_op jit(solution)/shard_map/schwarz_modes/pallas_call | solution.py:448
  46.6 3.8 %back_to_cells.1 = f32[32,256,128]{2,1,0:T(8,128)} custom-call(bf16[32,256,128]{2,1,0:T(8,128)(2,1)} %schwarz_modes.1.turned_far, bf16[256,256]{1,0:T(8,128)(2,1)} %constant.14.clone.more_0_.width_far), custom_call_target="tpu_custom_call" | custom-call | tf_op jit(solution)/shard_map/back_to_cells/pallas_call | solution.py:498

commit v4 on v3

--- a/solution.py
+++ b/solution.py
@@ -10,6 +10,7 @@
 from jax.sharding import PartitionSpec as P
 
 W = 8
+CORES = 2
 REFLECT = 0.6
 TIMESTEP = 64.0
 ZCHIPS = 8
@@ -76,9 +77,9 @@
 def run_front(
     pencils, previous, source, smalls_far, smalls, width, height, both, turns, heights_two, rowtab, modes,
     neighbor, depth, wall,
-    out, prev, src, slab, right, force, carry, iterate, waves, inbox, own, gath0, gath1, packet, zbox0, zbox1,
+    out, prev, src, slab, right, force, carry, iterate, waves, beside, pairs, inbox, ends, back, own, gath0, gath1, packet, zbox0, zbox1,
     rows, ghost, walls, picks, load_sem, slab_sem, small_sem, out_sem, x_send, x_recv, z_send, z_recv,
-    w_send, w_recv,
+    near_send, near_recv, far_send, far_recv, back_send, back_recv,
 ):
     gath = (gath0, gath1)
     zbox = (zbox0, zbox1)
@@ -97,7 +98,13 @@
 
     x_peers = [(lax.rem(cx + k, xchips)) * ZCHIPS + cz for k in range(1, xchips)]
     z_peers = [cx * ZCHIPS + lax.rem(cz + k, ZCHIPS) for k in range(1, ZCHIPS)]
-    w_peers = [lax.rem(pencil + k, pencils) for k in range(1, pencils)]
+    chips = pencils // CORES
+    core = lax.rem(pencil, CORES)
+    chip = pencil // CORES
+    sibling = pencil + 1 - 2 * core
+    far_peers = [lax.rem(chip + k, chips) * CORES + core for k in range(1, chips)]
+    w_peers = [sibling] + far_peers
+    pieces = columns // CORES // CHUNK
 
     barrier = pltpu.get_barrier_semaphore()
     for peer in x_peers + z_peers:
@@ -127,7 +134,7 @@
         for load in field_loads(c):
             load.start()
 
-    for load in small_loads:
+    for load in small_loads[:2]:
         load.wait()
     lists = [(f, t) for f in range(2) for t in range(segs)]
 
@@ -137,19 +144,19 @@
             for (f, t), d in zip(lists, found)
         )
 
-    depths = lax.fori_loop(0, boxes, search, tuple(jnp.int32(1) for _ in lists))
-
-    line = lax.broadcasted_iota(jnp.int32, (planes, heights), 0)
-    for f in range(2):
-        def mark(x, mask, f=f):
-            return jnp.where(line == x, wall[f, x], mask)
-
-        walls[f] = lax.fori_loop(0, planes, mark, jnp.zeros((planes, heights), jnp.int32))
+    depths = lax.fori_loop(0, boxes, search, tuple(jnp.int32(1) for _ in lists), unroll=8)
 
     chunks = columns // CHUNK
 
-    def chunk_at(c):
-        return pl.ds(c * CHUNK, CHUNK)
+    def place_of(s):
+        half_of = 1 - core if s < pieces else core
+        return half_of * pieces + s % pieces
+
+    def chunk_at(s):
+        return pl.ds(pl.multiple_of(place_of(s) * CHUNK, CHUNK), CHUNK)
+
+    def piece_at(h):
+        return pl.ds(h * CHUNK, CHUNK)
 
     def x_copies(it):
         return [
@@ -169,16 +176,30 @@
             for k in range(1, ZCHIPS)
         ]
 
-    def w_copies(it, c):
-        at = chunk_at(c)
+    def near_copy(it, s):
+        at = piece_at(s)
+        return pltpu.make_async_remote_copy(
+            waves.at[it, :, at], beside.at[it, :, at], near_send.at[it, s], near_recv.at[it, s],
+            device_id=(box, sibling), device_id_type=pl.DeviceIdType.MESH,
+        )
+
+    def far_copies(it, h):
+        at = piece_at(h)
         return [
             pltpu.make_async_remote_copy(
-                waves.at[it, (pencil + k) // pencils, at], inbox.at[it, k - 1, at],
-                w_send.at[it, c, k - 1], w_recv.at[it, c, k - 1],
-                device_id=(box, w_peers[k - 1]), device_id_type=pl.DeviceIdType.MESH,
+                pairs.at[it, (chip + k) // chips, at], inbox.at[it, k - 1, at],
+                far_send.at[it, h, k - 1], far_recv.at[it, h, k - 1],
+                device_id=(box, far_peers[k - 1]), device_id_type=pl.DeviceIdType.MESH,
             )
-            for k in range(1, pencils)
+            for k in range(1, chips)
         ]
+
+    def back_copy(it, h):
+        at = piece_at(h)
+        return pltpu.make_async_remote_copy(
+            ends.at[it, :, at], back.at[it, :, at], back_send.at[it, h], back_recv.at[it, h],
+            device_id=(box, sibling), device_id_type=pl.DeviceIdType.MESH,
+        )
 
     def forward_margins(it):
         for k in range(ZCHIPS):
@@ -211,6 +232,15 @@
     for copy in first_x:
         copy.start()
 
+    for load in small_loads[2:]:
+        load.wait()
+    line = lax.broadcasted_iota(jnp.int32, (planes, heights), 0)
+    for f in range(2):
+        def mark(x, mask, f=f):
+            return jnp.where(line == x, wall[f, x], mask)
+
+        walls[f] = lax.fori_loop(0, planes, mark, jnp.zeros((planes, heights), jnp.int32))
+
     def transform(x, _):
         now = prev[x]
         total = (now.astype(jnp.float32) + src[x].astype(jnp.float32)).astype(jnp.bfloat16)
@@ -252,6 +282,38 @@
     near_power = (2 * pencil + 1).astype(jnp.float32)
     far_power = (2 * pencils - 1 - 2 * pencil).astype(jnp.float32)
 
+    first_core = jnp.where(core == 0, 1.0, 0.0).astype(jnp.float32)
+    last_core = 1.0 - first_core
+
+    def join(it, h):
+        at = chunk_at(pieces + h)
+        near_copy(it, h).wait_recv()
+        decay = jnp.exp(modes[1, at])
+        mine = [waves[it, d, piece_at(pieces + h)].astype(jnp.float32) for d in range(2)]
+        theirs = [beside[it, d, piece_at(h)].astype(jnp.float32) for d in range(2)]
+        up = (first_core * decay + last_core) * mine[0] + (last_core * decay + first_core) * theirs[0]
+        down = (last_core * decay + first_core) * mine[1] + (first_core * decay + last_core) * theirs[1]
+        pairs[it, 0, piece_at(h)] = up.astype(jnp.bfloat16)
+        pairs[it, 1, piece_at(h)] = down.astype(jnp.bfloat16)
+        for copy in far_copies(it, h):
+            copy.start()
+
+    def reach_ends(it, h):
+        for copy in far_copies(it, h):
+            copy.wait_recv()
+        decay = jnp.exp(CORES * modes[1, chunk_at(pieces + h)])
+        low = jnp.zeros((CHUNK, heights), jnp.float32)
+        high = low
+        for k in range(chips - 1, 0, -1):
+            here = jnp.where(chip >= k, 1.0, 0.0).astype(jnp.float32)
+            low = here * inbox[it, k - 1, piece_at(h)].astype(jnp.float32) + decay * low
+        for k in range(1, chips):
+            here = jnp.where(chip >= k, 0.0, 1.0).astype(jnp.float32)
+            high = here * inbox[it, k - 1, piece_at(h)].astype(jnp.float32) + decay * high
+        ends[it, 0, piece_at(h)] = low.astype(jnp.bfloat16)
+        ends[it, 1, piece_at(h)] = high.astype(jnp.bfloat16)
+        back_copy(it, h).start()
+
     def sweep(it):
         def chunk(c):
             at = chunk_at(c)
@@ -268,34 +330,36 @@
             zero = jnp.zeros((CHUNK, heights), jnp.float32)
             up, down, _ = lax.fori_loop(0, planes, plane, (zero, zero, zero + 1.0), unroll=4)
             log = modes[1, at]
-            waves[it, 0, at] = (up - ratio * jnp.exp(log * near_power) * down).astype(jnp.bfloat16)
-            waves[it, 1, at] = (down - ratio * jnp.exp(log * far_power) * up).astype(jnp.bfloat16)
+            waves[it, 0, piece_at(c)] = (up - ratio * jnp.exp(log * near_power) * down).astype(jnp.bfloat16)
+            waves[it, 1, piece_at(c)] = (down - ratio * jnp.exp(log * far_power) * up).astype(jnp.bfloat16)
             loop = ratio * ratio * jnp.exp(log * (2 * pencils - 1))
             own[0, at] = loop * up - ratio * jnp.exp(log * (near_power - 1.0)) * down
             own[1, at] = loop * down - ratio * jnp.exp(log * (far_power - 1.0)) * up
-            for copy in w_copies(it, c):
-                copy.start()
+            near_copy(it, c).start()
 
         for c in range(chunks):
             chunk(c)
+            if c >= pieces:
+                join(it, c - pieces)
+        for h in range(pieces):
+            reach_ends(it, h)
 
     def solve(it, done):
         def chunk(c):
             at = chunk_at(c)
-            for copy in w_copies(it, c):
-                copy.wait_recv()
             ratio = modes[0, at]
             log = modes[1, at]
             weight = modes[2, at]
             decay = jnp.exp(log)
-            low = jnp.zeros((CHUNK, heights), jnp.float32)
-            high = low
-            for k in range(pencils - 1, 0, -1):
-                here = jnp.where(pencil >= k, 1.0, 0.0).astype(jnp.float32)
-                low = here * inbox[it, k - 1, at].astype(jnp.float32) + decay * low
-            for k in range(1, pencils):
-                here = jnp.where(pencil >= k, 0.0, 1.0).astype(jnp.float32)
-                high = here * inbox[it, k - 1, at].astype(jnp.float32) + decay * high
+            if c >= pieces:
+                outside = [ends[it, d, piece_at(c - pieces)].astype(jnp.float32) for d in range(2)]
+            else:
+                near_copy(it, c + pieces).wait_recv()
+                back_copy(it, c).wait_recv()
+                outside = [back[it, d, piece_at(c)].astype(jnp.float32) for d in range(2)]
+            near = [beside[it, d, piece_at((c + pieces) % chunks)].astype(jnp.float32) for d in range(2)]
+            low = last_core * near[0] + (last_core * decay + first_core) * outside[0]
+            high = first_core * near[1] + (first_core * decay + last_core) * outside[1]
             start = low + own[0, at] - ratio * jnp.exp(log * near_power) * high
             end = high + own[1, at] - ratio * jnp.exp(log * far_power) * low
 
@@ -322,7 +386,7 @@
             done(c, at)
 
         for c in range(chunks):
-            chunk(c)
+            chunk((c + pieces) % chunks)
 
     sweep(0)
 
@@ -339,7 +403,7 @@
         return jnp.concatenate([iterate[j, at], iterate[half + j, at]], axis=1)
 
     def take(c, at):
-        lhs = picks[c].astype(jnp.bfloat16)
+        lhs = picks[place_of(c)].astype(jnp.bfloat16)
         for j in range(half):
             rows[j] += jnp.dot(lhs, pair_of(j, at), preferred_element_type=jnp.float32)
 
@@ -379,27 +443,38 @@
     sweep(1)
 
     def to_cells(c, at):
+        there = piece_at(c)
         for j in range(half):
             cells = jnp.dot(pair_of(j, at), heights_two[...], preferred_element_type=jnp.float32)
-            src[j, at] = cells[:, :heights].astype(jnp.bfloat16)
-            src[half + j, at] = cells[:, heights:].astype(jnp.bfloat16)
-        pltpu.make_async_copy(src.at[:, at, :], out.at[:, at, :], out_sem.at[c]).start()
+            src[j, there] = cells[:, :heights].astype(jnp.bfloat16)
+            src[half + j, there] = cells[:, heights:].astype(jnp.bfloat16)
+        pltpu.make_async_copy(src.at[:, there, :], out.at[:, there, :], out_sem.at[c]).start()
 
     solve(1, to_cells)
 
     for c in range(chunks):
-        at = chunk_at(c)
+        at = piece_at(c)
         pltpu.make_async_copy(src.at[:, at, :], out.at[:, at, :], out_sem.at[c]).wait()
         for it in range(2):
-            for copy in w_copies(it, c):
+            near_copy(it, c).wait_send()
+    for it in range(2):
+        for h in range(pieces):
+            for copy in far_copies(it, h) + [back_copy(it, h)]:
                 copy.wait_send()
     for copy in first_x + first_z + second_x + second_z:
         copy.wait_send()
 
 
 def back_kernel(turned_far, width_far, solved_far, turned, width, solved, load_sem, width_sem, store_sem):
-    planes, _, heights = turned.shape
+    planes, columns, heights = turned.shape
     step = planes // LOADS
+    core = lax.rem(lax.axis_index("pencil"), CORES)
+    part_modes = columns // CORES
+    low = pl.ds(pl.multiple_of((1 - core) * part_modes, part_modes), part_modes)
+    high = pl.ds(pl.multiple_of(core * part_modes, part_modes), part_modes)
+
+    def pair_at(rows, x):
+        return jnp.concatenate([turned[x, rows], turned[x + 1, rows]], axis=1)
 
     def load(c):
         part = pl.ds(c * step, step)
@@ -419,7 +494,7 @@
         load(c).wait()
         for j in range(0, step, 2):
             x = c * step + j
-            pair = jnp.concatenate([turned[x], turned[x + 1]], axis=1)
+            pair = jnp.concatenate([pair_at(low, x), pair_at(high, x)], axis=0)
             full = jnp.dot(width[...], pair, preferred_element_type=jnp.float32)
             solved[x] = full[:, :heights]
             solved[x + 1] = full[:, heights:]
@@ -465,7 +540,11 @@
             pltpu.VMEM(field, jnp.float32),
             pltpu.VMEM(field, jnp.bfloat16),
             pltpu.VMEM((2, 2, columns, heights), jnp.bfloat16),
-            pltpu.VMEM((2, pencils - 1, columns, heights), jnp.bfloat16),
+            pltpu.VMEM((2, 2, columns, heights), jnp.bfloat16),
+            pltpu.VMEM((2, 2, columns // CORES, heights), jnp.bfloat16),
+            pltpu.VMEM((2, pencils // CORES - 1, columns // CORES, heights), jnp.bfloat16),
+            pltpu.VMEM((2, 2, columns // CORES, heights), jnp.bfloat16),
+            pltpu.VMEM((2, 2, columns // CORES, heights), jnp.bfloat16),
             pltpu.VMEM((2, columns, heights), jnp.float32),
             pltpu.VMEM((xchips, lists) + block, jnp.bfloat16),
             pltpu.VMEM((xchips, lists) + block, jnp.bfloat16),
@@ -484,8 +563,12 @@
             dma((2, xchips - 1)),
             dma((2, ZCHIPS - 1)),
             dma((2, ZCHIPS - 1)),
-            dma((2, columns // CHUNK, pencils - 1)),
-            dma((2, columns // CHUNK, pencils - 1)),
+            dma((2, columns // CHUNK)),
+            dma((2, columns // CHUNK)),
+            dma((2, columns // CORES // CHUNK, pencils // CORES - 1)),
+            dma((2, columns // CORES // CHUNK, pencils // CORES - 1)),
+            dma((2, columns // CORES // CHUNK)),
+            dma((2, columns // CORES // CHUNK)),
         ],
         compiler_params=pltpu.CompilerParams(
             collective_id=0, has_side_effects=True, vmem_limit_bytes=67_043_328

time: 50.5 us -> 51.3 us (1.016)
  Pallas kernels: 50.4 us -> 51.1 us
    pallas_call x1, Pallas kernels: 46.6 us -> 47.4 us  [shards(): pl.pallas_call(functools.partial(front_kernel, pencils), out_shape=jax.Sh...]
where the time goes in v4:
time: 51.3 us; the launch traced here: 51.2 us
  Pallas kernels  51.1 us (100%)
    pallas_call x1, Pallas kernels, shards(): pl.pallas_call(functools.partial(front_kernel, pencils), out_shape=jax.Sh...  47.4 us
    pallas_call x1, Pallas kernels, shards(): pl.pallas_call(back_kernel, out_shape=jax.ShapeDtypeStruct(field, jnp.flo...  3.77 us

profile of v4, /device:TPU:1, one launch (start us, length us, event | category | flops | bytes accessed | tf_op | source)
XLA Modules:
  0.0 51.2 jit_solution(2389872576391211033)
XLA Ops:
  0.0 47.4 %schwarz_modes.1.turned_far = bf16[32,256,128]{2,1,0:T(8,128)(2,1)} custom-call(bf16[32,256,128]{2,1,0:T(8,128)(2,1)} %bitcast.6, bf16[32,256,128]{2,1,0:T(8,128)(2,1)} %bitcast.7, s32[2,16,32]{2,1,0:T(8,128)} %bitcast.8, s32[2,16,32]{2,1,0:T(8,128)} %bitcast.9, s32[2,32]{1,0:T(2,128)} %bitcast.10, bf16[256,256]{1,0:T(8,128)(2,1)} %constant.14.clone.more_0_.width_far, ...), custom_call_target="tpu_custom_call" | custom-call | tf_op jit(solution)/shard_map/schwarz_modes/pallas_call | solution.py:523
  47.4 3.8 %back_to_cells.1 = f32[32,256,128]{2,1,0:T(8,128)} custom-call(bf16[32,256,128]{2,1,0:T(8,128)(2,1)} %schwarz_modes.1.turned_far, bf16[256,256]{1,0:T(8,128)(2,1)} %constant.14.clone.more_0_.width_far), custom_call_target="tpu_custom_call" | custom-call | tf_op jit(solution)/shard_map/back_to_cells/pallas_call | solution.py:581
